TPU v7x, 128 devices: a whole 4x4x4 slice. The times are simulated.
128 devices in a mesh: space: 16 (over y_hi, x, core), code: 4 (over z), clip: 2 (over y_lo).
Axes of the slice: x: 4, y: 4 (y_hi: 2, y_lo: 2; y = y_hi * 2 + y_lo), z: 4, core: 2. Of those that a mesh axis runs over, the one named last changes fastest.
Arguments:
- soft_weights: bfloat16 [2, 1024, 32, 8192], P('clip', 'space', None, 'code'), may hold values from 0.00029945374 to 0.029907227
- codebook: bfloat16 [8192, 256], P('code'), may hold values from -6 to 6
- kernel_one: bfloat16 [3, 3, 256, 512], replicated, may hold values from -0.125 to 0.125
- kernel_two: bfloat16 [3, 3, 512, 512], replicated, may hold values from -0.09375 to 0.09375
- cotangent: bfloat16 [2, 1024, 32, 512], P('clip', ('space', 'code')), may hold values from -16 to 16
Outputs:
- decoded: bfloat16 [2, 1024, 32, 512], P('clip', ('space', 'code'))
- grad_one: float32 [3, 3, 256, 512], P(None, None, None, ('space', 'code', 'clip'))
- grad_two: float32 [3, 3, 512, 512], P(None, None, None, ('space', 'code', 'clip'))
- grad_codebook: float32 [8192, 256], P('code')
All inputs are finite; a program needn't handle non-finite values.
Results may differ from a plain program's by a relative error of at most 0.02.
Values may be sent and summed in bfloat16 or wider, within the bound.
A program may use at most 192 MiB of HBM per device.

v0:
```python
import jax
import jax.numpy as jnp
from jax import lax
from jax.sharding import PartitionSpec as P


def with_halo(block, sides, width):
    for axis, dim in sides:
        count = lax.axis_size(axis)
        forward = [(i, i + 1) for i in range(count - 1)]
        backward = [(target, source) for source, target in forward]
        low = lax.ppermute(
            lax.slice_in_dim(block, block.shape[dim] - width, None, axis=dim), axis, forward
        )
        high = lax.ppermute(lax.slice_in_dim(block, 0, width, axis=dim), axis, backward)
        block = jnp.concatenate([low, block, high], axis=dim)
    return block


def extend(field):
    grown = with_halo(field, ((("space", "code"), 0),), 1)
    return jnp.pad(grown, ((0, 0), (1, 1), (0, 0)))


def taps_forward(padded, kernel):
    height = padded.shape[0] - 2
    breadth = padded.shape[1] - 2
    accum = jnp.zeros((height * breadth, kernel.shape[3]), jnp.float32)
    for first in range(3):
        for second in range(3):
            window = padded[first : first + height, second : second + breadth].reshape(
                height * breadth, -1
            )
            accum = accum + jnp.dot(
                window, kernel[first, second], preferred_element_type=jnp.float32
            )
    return accum.reshape(height, breadth, -1)


def taps_back(padded, kernel):
    height = padded.shape[0] - 2
    breadth = padded.shape[1] - 2
    accum = jnp.zeros((height * breadth, kernel.shape[2]), jnp.float32)
    for first in range(3):
        for second in range(3):
            window = padded[
                2 - first : 2 - first + height, 2 - second : 2 - second + breadth
            ].reshape(height * breadth, -1)
            accum = accum + jnp.dot(
                window, kernel[first, second].T, preferred_element_type=jnp.float32
            )
    return accum.reshape(height, breadth, -1)


def kernel_grad(padded, upstream):
    height = upstream.shape[0]
    breadth = upstream.shape[1]
    flat_up = upstream.reshape(height * breadth, -1)
    result = []
    for first in range(3):
        line = []
        for second in range(3):
            window = padded[first : first + height, second : second + breadth].reshape(
                height * breadth, -1
            )
            line.append(
                lax.dot_general(
                    window, flat_up, (((0,), (0,)), ((), ())), preferred_element_type=jnp.float32
                )
            )
        result.append(jnp.stack(line))
    return jnp.stack(result)


def on_device(soft_weights, codebook, kernel_one, kernel_two, cotangent):
    weights = soft_weights[0]
    upstream = cotangent[0]
    own_rows = upstream.shape[0]
    breadth = weights.shape[1]
    code_slice = weights.shape[2]
    partial_value = jnp.dot(
        weights.reshape(-1, code_slice), codebook, preferred_element_type=jnp.float32
    )
    partial_value = partial_value.reshape(weights.shape[0], breadth, -1)
    summed = lax.psum(partial_value, "code")
    owned = lax.dynamic_slice_in_dim(summed, lax.axis_index("code") * own_rows, own_rows, 0)
    embedded = owned.astype(jnp.bfloat16)
    embed_pad = extend(embedded)
    pre_one = taps_forward(embed_pad, kernel_one)
    hidden = jax.nn.silu(pre_one).astype(jnp.bfloat16)
    hidden_pad = extend(hidden)
    decoded = taps_forward(hidden_pad, kernel_two).astype(jnp.bfloat16)
    grad_hidden = taps_back(extend(upstream), kernel_two)
    sigma = jax.nn.sigmoid(pre_one)
    grad_pre = (grad_hidden * sigma * (1.0 + pre_one * (1.0 - sigma))).astype(jnp.bfloat16)
    grad_embedded = taps_back(extend(grad_pre), kernel_one).astype(jnp.bfloat16)
    piece = lax.all_gather(grad_embedded, "code", axis=0, tiled=True)
    code_terms = lax.dot_general(
        weights.reshape(-1, code_slice),
        piece.reshape(-1, piece.shape[2]),
        (((0,), (0,)), ((), ())),
        preferred_element_type=jnp.float32,
    )
    grad_codebook = lax.psum(code_terms.astype(jnp.bfloat16), ("space", "clip")).astype(jnp.float32)
    term_two = kernel_grad(hidden_pad, upstream)
    term_one = kernel_grad(embed_pad, grad_pre)
    grad_one, grad_two = (
        lax.psum_scatter(term_one, ("space", "code", "clip"), scatter_dimension=3, tiled=True),
        lax.psum_scatter(term_two, ("space", "code", "clip"), scatter_dimension=3, tiled=True),
    )
    return (decoded[None], grad_one, grad_two, grad_codebook)


def solution(mesh):
    in_specs = (
        P("clip", "space", None, "code"),
        P("code", None),
        P(),
        P(),
        P("clip", ("space", "code"), None, None),
    )
    out_specs = (
        P("clip", ("space", "code"), None, None),
        P(None, None, None, ("space", "code", "clip")),
        P(None, None, None, ("space", "code", "clip")),
        P("code", None),
    )
    return jax.shard_map(
        on_device, mesh=mesh, in_specs=in_specs, out_specs=out_specs, check_vma=False
    )
```

profile of v0, /device:TPU:1, one launch (start us, length us, event | category | flops | bytes accessed | tf_op | source)
XLA Modules:
  0.0 509.3 jit_solution(13997313864569233537)
XLA Ops:
  7.2 1.2 copy-done
  8.4 5.7 %fusion = f32[64,32,256]{2,1,0:T(8,128)S(1)} fusion(bf16[1,64,32,2048]{3,2,1,0:T(8,128)(2,1)} %param.5, bf16[2048,256]{1,0:T(8,128)(2,1)S(1)} %copy-done), kind=kOutput, calls=%fused_computation.1 | convolution fusion | flops 2147483648 | bytes 11534336 | tf_op jit(solution)/shard_map/dot_general | solution.py:81
  14.1 44.1 %all-reduce.14 = bf16[64,32,256]{2,1,0:T(8,128)(2,1)} all-reduce(f32[64,32,256]{2,1,0:T(8,128)S(1)} %fusion), channel_id=1, replica_groups=mesh['space'=16,'code'=4,'clip'=2] {'code'}, use_global_device_ids=true, to_apply=%region_0.0 | all-reduce | flops 524288 | bytes 3145728 | tf_op jit(solution)/shard_map/psum | solution.py:85
  58.3 1.1 dynamic-slice_convert_fusion
  59.4 1.9 collective-permute-start
  61.3 5.2 %collective-permute-start.1 = (bf16[1,32,256]{2,1,0:T(8,128)(2,1)S(1)}, bf16[1,32,256]{2,1,0:T(8,128)(2,1)S(1)}, u32[]{:S(2)}, u32[]{:S(2)}) collective-permute-start(bf16[1,32,256]{2,1,0:T(8,128)(2,1)S(1)} %get-tuple-element.55), channel_id=1, source_target_pairs={{2,0},{4,2},{6,4},{8,6},{10,8},{12,10},{14,12},{16,14},{18,16},{20... | collective-permute-start | bytes 49160 | tf_op jit(solution)/shard_map/ppermute | solution.py:15
  66.5 1.9 collective-permute-start.4
  68.5 4.9 collective-permute-start.5
  76.5 1.5 convolution_bitcast_fusion.4
  78.3 0.5 fusion.113
  78.8 0.6 slice-done
  84.6 0.7 fusion.115
  87.6 0.6 fusion.116
  88.3 1.9 collective-permute-start.2
  90.2 4.9 collective-permute-start.3
  95.0 1.9 collective-permute-start.6
  97.0 5.0 collective-permute-start.7
  103.2 2.7 pad_maximum_fusion.1
  105.8 7.3 %copy.12 = f32[3,3,256,512]{2,1,0,3:T(4,128)} copy(f32[3,3,256,512]{3,2,1,0:T(8,128)} %pad_maximum_fusion.1) | data formatting | bytes 9437184 | tf_op jit(solution)/shard_map/stack | solution.py:72
  113.4 2.0 fusion.114
  118.1 0.6 convolution_add_fusion.24
  119.7 1.1 fusion.9
  121.4 1.4 convolution_bitcast_fusion.1
  123.4 1.4 convolution_bitcast_fusion.2
  126.3 1.4 convolution_bitcast_fusion
  127.8 3.4 maximum_bitcast_fusion
  131.2 27.6 %all-gather.2.cloned.1.call-done = bf16[64,32,256]{2,1,0:T(8,128)(2,1)} async-done(((bf16[16,32,256]{2,1,0:T(8,128)(2,1)}), bf16[64,32,256]{2,1,0:T(8,128)(2,1)}) %all-gather.2.cloned.1.call-update) | async-done | bytes 1048592 | tf_op jit(solution)/shard_map/all_gather | solution.py:97
  158.8 7.0 %fusion.2 = bf16[2048,256]{0,1:T(8,128)(2,1)} fusion(bf16[2048,256]{1,0:T(8,128)(2,1)} %bitcast.297, bf16[2048,2048]{1,0:T(8,128)(2,1)} %bitcast.275), kind=kOutput, calls=%fused_computation.8 | convolution fusion | flops 2148007936 | bytes 10485760 | tf_op jit(solution)/shard_map/dot_general | solution.py:98
  166.1 2.3 maximum_bitcast_fusion.2
  168.9 1.0 copy-done.4
  169.9 4.7 pad_maximum_fusion
  174.6 13.8 %copy.13 = f32[3,3,512,512]{2,1,0,3:T(4,128)} copy(f32[3,3,512,512]{3,2,1,0:T(8,128)} %pad_maximum_fusion) | data formatting | bytes 18874368 | tf_op jit(solution)/shard_map/stack | solution.py:72
  188.5 1.7 fusion.32
  190.2 1.5 fusion.14
  191.7 1.5 convolution_add_fusion.13
  193.2 1.5 convolution_add_fusion.12
  194.7 1.6 convolution_add_fusion.11
  196.3 1.5 convolution_add_fusion.10
  197.8 1.5 convolution_add_fusion.9
  199.3 1.5 convolution_add_fusion.8
  200.8 2.4 fusion.7
  203.2 70.1 %all-reduce.11.cloned.1.call-done = bf16[2048,256]{0,1:T(8,128)(2,1)} async-done(((bf16[2048,256]{0,1:T(8,128)(2,1)}), bf16[2048,256]{0,1:T(8,128)(2,1)}) %all-reduce.11.cloned.1.call-update) | async-done | bytes 1048592 | tf_op jit(solution)/shard_map/psum | solution.py:104
  273.2 2.6 copy.16
  275.8 223.9 %all-reduce.13.cloned.1.call-done = (f32[3,3,256,512]{2,1,0,3:T(4,128)}, f32[3,3,512,512]{2,1,0,3:T(4,128)}) async-done(((f32[3,3,256,512]{2,1,0,3:T(4,128)}, f32[3,3,512,512]{2,1,0,3:T(4,128)}), (f32[3,3,256,512]{2,1,0,3:T(4,128)}, f32[3,3,512,512]{2,1,0,3:T(4,128)})) %all-reduce.13.cloned.1.call-update) | async-done | bytes 14155792
  499.7 0.8 constant_dynamic-slice_fusion.1
  500.5 0.9 constant_dynamic-slice_fusion
  501.5 0.7 copy.15
  502.1 0.6 copy.14
  (120 shorter events, 19.2 us)
Async XLA Ops:
  7.2 1.2 copy-start
  7.2 151.6 %all-gather.2.cloned.1.call-start = ((), (), s32[]{:S(2)}) async-start(), calls=%async_computation | async-start | bytes 1310720 | tf_op jit(solution)/shard_map/all_gather | solution.py:97
  14.1 52.4 %copy-start.2 = (bf16[1,16,32,512]{3,2,1,0:T(8,128)(2,1)S(1)}, bf16[1,16,32,512]{3,2,1,0:T(8,128)(2,1)}, u32[]{:S(2)}) copy-start(bf16[1,16,32,512]{3,2,1,0:T(8,128)(2,1)} %param.9) | copy-start | bytes 1572868
  58.3 15.5 %copy-start.5 = (bf16[3,3,256,512]{3,2,1,0:T(8,128)(2,1)S(1)}, bf16[3,3,256,512]{3,2,1,0:T(8,128)(2,1)}, u32[]{:S(2)}) copy-start(bf16[3,3,256,512]{3,2,1,0:T(8,128)(2,1)} %param.7) | copy-start | bytes 7077892
  59.4 13.9 %collective-permute-start = (bf16[1,32,256]{2,1,0:T(8,128)(2,1)S(1)}, bf16[1,32,256]{2,1,0:T(8,128)(2,1)S(1)}, u32[]{:S(2)}, u32[]{:S(2)}) collective-permute-start(bf16[1,32,256]{2,1,0:T(8,128)(2,1)S(1)} %get-tuple-element.54), channel_id=1, source_target_pairs={{0,2},{2,4},{4,6},{6,8},{8,10},{10,12},{12,14},{14,16},{16,18},{18... | collective-permute-start | bytes 49160 | tf_op jit(solution)/shard_map/ppermute | solution.py:12
  61.3 12.0 %collective-permute-start.1 = (bf16[1,32,256]{2,1,0:T(8,128)(2,1)S(1)}, bf16[1,32,256]{2,1,0:T(8,128)(2,1)S(1)}, u32[]{:S(2)}, u32[]{:S(2)}) collective-permute-start(bf16[1,32,256]{2,1,0:T(8,128)(2,1)S(1)} %get-tuple-element.55), channel_id=1, source_target_pairs={{2,0},{4,2},{6,4},{8,6},{10,8},{12,10},{14,12},{16,14},{18,16},{20... | collective-permute-start | bytes 49160 | tf_op jit(solution)/shard_map/ppermute | solution.py:15
  66.5 11.5 %collective-permute-start.4 = (bf16[1,32,512]{2,1,0:T(8,128)(2,1)S(1)}, bf16[1,32,512]{2,1,0:T(8,128)(2,1)S(1)}, u32[]{:S(2)}, u32[]{:S(2)}) collective-permute-start(bf16[1,32,512]{2,1,0:T(8,128)(2,1)S(1)} %get-tuple-element.40), channel_id=1, source_target_pairs={{0,2},{2,4},{4,6},{6,8},{8,10},{10,12},{12,14},{14,16},{16,18},{18... | collective-permute-start | bytes 98312 | tf_op jit(solution)/shard_map/ppermute | solution.py:12
  68.5 9.6 %collective-permute-start.5 = (bf16[1,32,512]{2,1,0:T(8,128)(2,1)S(1)}, bf16[1,32,512]{2,1,0:T(8,128)(2,1)S(1)}, u32[]{:S(2)}, u32[]{:S(2)}) collective-permute-start(bf16[1,32,512]{2,1,0:T(8,128)(2,1)S(1)} %get-tuple-element.41), channel_id=1, source_target_pairs={{2,0},{4,2},{6,4},{8,6},{10,8},{12,10},{14,12},{16,14},{18,16},{20... | collective-permute-start | bytes 98312 | tf_op jit(solution)/shard_map/ppermute | solution.py:15
  76.5 7.6 %copy-start.19 = (f32[512,512]{1,0:T(8,128)}, f32[512,512]{1,0:T(8,128)S(1)}, u32[]{:S(2)}) copy-start(f32[512,512]{1,0:T(8,128)S(1)} %fusion.6) | copy-start | bytes 3145732
  76.5 2.9 slice-start
  78.0 1.7 slice-start.1
  84.1 1.6 copy-start.22
  84.6 3.0 copy-start.6
  84.6 17.8 %copy-start.8 = (bf16[16,32,512]{2,1,0:T(8,128)(2,1)}, bf16[16,32,512]{2,1,0:T(8,128)(2,1)S(1)}, u32[]{:S(2)}) copy-start(bf16[16,32,512]{2,1,0:T(8,128)(2,1)S(1)} %get-tuple-element.14) | copy-start | bytes 1572868
  88.3 24.8 %collective-permute-start.2 = (bf16[1,32,512]{2,1,0:T(8,128)(2,1)}, bf16[1,32,512]{2,1,0:T(8,128)(2,1)S(1)}, u32[]{:S(2)}, u32[]{:S(2)}) collective-permute-start(bf16[1,32,512]{2,1,0:T(8,128)(2,1)} %get-tuple-element.44), channel_id=1, source_target_pairs={{0,2},{2,4},{4,6},{6,8},{8,10},{10,12},{12,14},{14,16},{16,18},{18... | collective-permute-start | bytes 98312 | tf_op jit(solution)/shard_map/ppermute | solution.py:12
  90.2 22.9 %collective-permute-start.3 = (bf16[1,32,512]{2,1,0:T(8,128)(2,1)}, bf16[1,32,512]{2,1,0:T(8,128)(2,1)S(1)}, u32[]{:S(2)}, u32[]{:S(2)}) collective-permute-start(bf16[1,32,512]{2,1,0:T(8,128)(2,1)} %get-tuple-element.45), channel_id=1, source_target_pairs={{2,0},{4,2},{6,4},{8,6},{10,8},{12,10},{14,12},{16,14},{18,16},{20... | collective-permute-start | bytes 98312 | tf_op jit(solution)/shard_map/ppermute | solution.py:15
  95.0 20.3 %collective-permute-start.6 = (bf16[1,32,512]{2,1,0:T(8,128)(2,1)}, bf16[1,32,512]{2,1,0:T(8,128)(2,1)S(1)}, u32[]{:S(2)}, u32[]{:S(2)}) collective-permute-start(bf16[1,32,512]{2,1,0:T(8,128)(2,1)} %get-tuple-element.36), channel_id=1, source_target_pairs={{0,2},{2,4},{4,6},{6,8},{8,10},{10,12},{12,14},{14,16},{16,18},{18... | collective-permute-start | bytes 98312 | tf_op jit(solution)/shard_map/ppermute | solution.py:12
  97.0 18.4 %collective-permute-start.7 = (bf16[1,32,512]{2,1,0:T(8,128)(2,1)}, bf16[1,32,512]{2,1,0:T(8,128)(2,1)S(1)}, u32[]{:S(2)}, u32[]{:S(2)}) collective-permute-start(bf16[1,32,512]{2,1,0:T(8,128)(2,1)} %get-tuple-element.37), channel_id=1, source_target_pairs={{2,0},{4,2},{6,4},{8,6},{10,8},{12,10},{14,12},{16,14},{18,16},{20... | collective-permute-start | bytes 98312 | tf_op jit(solution)/shard_map/ppermute | solution.py:15
  105.8 7.3 %copy-start.7 = (bf16[16,32,512]{2,1,0:T(8,128)(2,1)S(1)}, bf16[16,32,512]{2,1,0:T(8,128)(2,1)}, u32[]{:S(2)}) copy-start(bf16[16,32,512]{2,1,0:T(8,128)(2,1)} %copy-done.6) | copy-start | bytes 1572868
  113.4 2.0 copy-start.9
  116.6 1.2 copy-start.20
  116.6 1.5 copy-start.23
  120.8 152.5 %all-reduce.11.cloned.1.call-start = ((), (), s32[]{:S(2)}) async-start(), calls=%async_computation.1 | async-start | bytes 2097152 | tf_op jit(solution)/shard_map/psum | solution.py:104
  120.9 2.4 copy-start.17
  120.9 1.9 copy-start.11
  121.4 1.9 copy-start.10
  122.9 1.9 copy-start.12
  123.3 1.9 copy-start.13
  124.8 1.0 copy-start.16
  125.3 1.1 copy-start.14
  125.7 2.0 copy-start.24
  165.8 333.9 %all-reduce.13.cloned.1.call-start = ((), (), s32[]{:S(2)}) async-start(), calls=%async_computation.2 | async-start | bytes 37748736
  166.1 2.8 copy-start.3
  166.1 3.8 copy-start.4
  188.5 1.7 copy-start.15
  188.5 3.2 copy-start.18
  194.7 1.6 copy-start.21
  200.8 302.0 %copy-start.1 = (bf16[2048,256]{1,0:T(8,128)(2,1)S(1)}, bf16[2048,256]{1,0:T(8,128)(2,1)}, u32[]{:S(2)}) copy-start(bf16[2048,256]{1,0:T(8,128)(2,1)} %param.6) | copy-start | bytes 3145732
Sparse Core Ops, SparseCore 0:
  120.9 37.8 all-gather.1
  166.0 107.2 all-reduce.10
  278.8 220.8 all-reduce.12
where the time goes:
time: 511 us; the launch traced here: 509 us
  waiting for transfers between devices  322 us (63%)
  matrix products  49.1 us (10%)
  blocking collectives  44.1 us (9%)
  local copies, waits for them, and re-layouts  36.6 us (7%)
  starting transfers between devices  27.9 us (5%)
  other arithmetic  15.2 us (3%)
  between operations  14.6 us (3%)
    unnamed x4, waiting for transfers between devices  224 us
    psum x1, waiting for transfers between devices, on_device(): lax.psum(code_terms.astype(jnp.bfloat16), ('space', 'clip'))  70.1 us
    psum x1, blocking collectives, on_device(): summed = lax.psum(partial_value, 'code')  44.1 us
    all_gather x1, waiting for transfers between devices, on_device(): piece = lax.all_gather(grad_embedded, 'code', axis=0, tiled=True)  27.6 us
    another operation x2, local copies, waits for them, and re-layouts, kernel_grad(): return jnp.stack(result)  21.1 us
    ppermute x4, starting transfers between devices, with_halo(): lax.ppermute(lax.slice_in_dim(block, 0, width, axis=dim), axis, backward)  19.9 us
    dot_general x18, matrix products, taps_forward(): jnp.dot(window, kernel[first, second], preferred_element_type=jnp.float32)  17.2 us
    another operation x6, other arithmetic, kernel_grad(): return jnp.stack(result)  13.6 us
  transfers between devices with their start and end apart: 11, of which 3 were waited for; matrix products, arithmetic and copies ran while one was open for 13% of the time, Pallas kernels for 0%

commit v1 on v0

--- a/solution.py
+++ b/solution.py
@@ -2,6 +2,11 @@
 import jax.numpy as jnp
 from jax import lax
 from jax.sharding import PartitionSpec as P
+from jax.lax import all_gather
+
+
+def _guide_sectors(field_in, shard_axis):
+    return jnp.sum(all_gather(field_in, axis_name=shard_axis), axis=0)
 
 
 def with_halo(block, sides, width):
@@ -82,7 +87,7 @@
         weights.reshape(-1, code_slice), codebook, preferred_element_type=jnp.float32
     )
     partial_value = partial_value.reshape(weights.shape[0], breadth, -1)
-    summed = lax.psum(partial_value, "code")
+    summed = _guide_sectors(partial_value, "code")
     owned = lax.dynamic_slice_in_dim(summed, lax.axis_index("code") * own_rows, own_rows, 0)
     embedded = owned.astype(jnp.bfloat16)
     embed_pad = extend(embedded)

time: 511 us -> 544 us (1.065)
  waiting for transfers between devices: 322 us -> 386 us
  blocking collectives: 44.1 us -> 0 us
  other arithmetic: 15.2 us -> 20.8 us
    all_gather x0 -> x1, waiting for transfers between devices: none -> 68.7 us  [_guide_sectors(): return jnp.sum(all_gather(field_in, axis_name=shard_axis), axis=0)]
    psum x1 -> x0, blocking collectives: 44.1 us -> none  [on_device(): summed = lax.psum(partial_value, 'code')]
    all_gather x1, waiting for transfers between devices: 27.6 us -> 21.7 us  [on_device(): piece = lax.all_gather(grad_embedded, 'code', axis=0, tiled=True)]
    reduce_sum x0 -> x1, other arithmetic: none -> 5.64 us  [_guide_sectors(): return jnp.sum(all_gather(field_in, axis_name=shard_axis), axis=0)]
    unnamed x59 -> x49, local copies, waits for them, and re-layouts: 9.85 us -> 14.1 us
    unnamed x4 -> x5, waiting for transfers between devices: 224 us -> 224 us
  transfers between devices with their start and end apart: 11 -> 12, of which waited for: 3 -> 5; matrix products, arithmetic and copies ran while one was open for 13% -> 13% of each run, Pallas kernels for 0% -> 0%
where the time goes in v1:
time: 544 us; the launch traced here: 542 us
  waiting for transfers between devices  386 us (71%)
  matrix products  52.9 us (10%)
  local copies, waits for them, and re-layouts  38.9 us (7%)
  starting transfers between devices  29.7 us (5%)
  other arithmetic  20.8 us (4%)
  between operations  14.5 us (3%)
    unnamed x5, waiting for transfers between devices  224 us
    psum x1, waiting for transfers between devices, on_device(): lax.psum(code_terms.astype(jnp.bfloat16), ('space', 'clip'))  70.3 us
    all_gather x1, waiting for transfers between devices, _guide_sectors(): return jnp.sum(all_gather(field_in, axis_name=shard_axis), axis=0)  68.7 us
    all_gather x1, waiting for transfers between devices, on_device(): piece = lax.all_gather(grad_embedded, 'code', axis=0, tiled=True)  21.7 us
    another operation x2, local copies, waits for them, and re-layouts, kernel_grad(): return jnp.stack(result)  20.9 us
    ppermute x4, starting transfers between devices, with_halo(): lax.ppermute(lax.slice_in_dim(block, 0, width, axis=dim), axis, backward)  18.1 us
    dot_general x18, matrix products, taps_forward(): jnp.dot(window, kernel[first, second], preferred_element_type=jnp.float32)  17.2 us
    unnamed x49, local copies, waits for them, and re-layouts  14.1 us
  transfers between devices with their start and end apart: 12, of which 5 were waited for; matrix products, arithmetic and copies ran while one was open for 13% of the time, Pallas kernels for 0%

profile of v1, /device:TPU:1, one launch (start us, length us, event | category | flops | bytes accessed | tf_op | source)
XLA Modules:
  0.0 542.3 jit_solution(2941947368784613855)
XLA Ops:
  7.2 1.2 copy-done
  8.4 7.1 %fusion = f32[64,32,256]{2,1,0:T(8,128)} fusion(bf16[1,64,32,2048]{3,2,1,0:T(8,128)(2,1)} %param.5, bf16[2048,256]{1,0:T(8,128)(2,1)S(1)} %copy-done), kind=kOutput, calls=%fused_computation.1 | convolution fusion | flops 2147483648 | bytes 11534336 | tf_op jit(solution)/shard_map/dot_general | solution.py:86
  15.6 4.4 collective-permute-start.4
  19.9 4.6 collective-permute-start.5
  24.5 1.0 collective-permute-done.5
  26.4 2.1 copy-done.3
  29.0 1.4 fusion.12
  33.3 68.7 %all-gather.6.cloned.1.call-done = f32[256,32,256]{2,1,0:T(8,128)} async-done(((f32[64,32,256]{2,1,0:T(8,128)}), f32[256,32,256]{2,1,0:T(8,128)}) %all-gather.6.cloned.1.call-update) | async-done | bytes 8388624 | tf_op jit(solution)/shard_map/all_gather | solution.py:9
  102.0 5.6 %reduce_sum.9 = bf16[64,32,256]{2,1,0:T(8,128)(2,1)} reduce(f32[4,64,32,256]{3,2,1,0:T(8,128)} %bitcast.277, f32[]{:T(128)} %constant.4.clone.1), dimensions={0}, to_apply=%region_0.0 | reduce | flops 1572864 | bytes 9437188 | tf_op jit(solution)/shard_map/reduce_sum | solution.py:9
  107.6 1.0 dynamic-slice_convert_fusion
  108.6 3.0 collective-permute-start
  111.6 3.8 collective-permute-start.1
  115.4 1.9 fusion.4
  117.6 1.6 copy-done.6
  122.0 1.5 convolution_bitcast_fusion.4
  126.4 1.9 collective-permute-start.2
  128.3 4.9 collective-permute-start.3
  133.2 1.9 collective-permute-start.6
  135.1 4.9 collective-permute-start.7
  141.1 2.7 pad_maximum_fusion.1
  143.7 7.2 %copy.12 = f32[3,3,256,512]{2,1,0,3:T(4,128)} copy(f32[3,3,256,512]{3,2,1,0:T(8,128)} %pad_maximum_fusion.1) | data formatting | bytes 9437184 | tf_op jit(solution)/shard_map/stack | solution.py:77
  151.2 1.6 fusion.114
  153.6 1.1 copy-done.7
  158.3 1.0 fusion.9
  160.3 1.5 convolution_bitcast_fusion.1
  162.3 1.4 convolution_bitcast_fusion.2
  165.3 1.4 convolution_bitcast_fusion
  166.7 3.4 maximum_bitcast_fusion
  170.1 21.7 %all-gather.4.cloned.1.call-done = bf16[64,32,256]{2,1,0:T(8,128)(2,1)} async-done(((bf16[16,32,256]{2,1,0:T(8,128)(2,1)}), bf16[64,32,256]{2,1,0:T(8,128)(2,1)}) %all-gather.4.cloned.1.call-update) | async-done | bytes 1048592 | tf_op jit(solution)/shard_map/all_gather | solution.py:102
  191.8 7.0 %fusion.2 = bf16[2048,256]{0,1:T(8,128)(2,1)} fusion(bf16[2048,256]{1,0:T(8,128)(2,1)} %bitcast.297, bf16[2048,2048]{1,0:T(8,128)(2,1)} %bitcast.276), kind=kOutput, calls=%fused_computation.8 | convolution fusion | flops 2148007936 | bytes 10485760 | tf_op jit(solution)/shard_map/dot_general | solution.py:103
  199.1 2.3 maximum_bitcast_fusion.2
  201.9 1.0 copy-done.5
  202.9 4.7 pad_maximum_fusion
  207.6 13.7 %copy.13 = f32[3,3,512,512]{2,1,0,3:T(4,128)} copy(f32[3,3,512,512]{3,2,1,0:T(8,128)} %pad_maximum_fusion) | data formatting | bytes 18874368 | tf_op jit(solution)/shard_map/stack | solution.py:77
  221.3 1.7 fusion.32
  223.0 1.5 fusion.14
  224.5 1.5 convolution_add_fusion.13
  226.0 1.5 convolution_add_fusion.12
  227.5 1.6 convolution_add_fusion.11
  229.1 1.5 convolution_add_fusion.10
  230.6 1.5 convolution_add_fusion.9
  232.1 1.5 convolution_add_fusion.8
  233.6 2.4 fusion.7
  236.0 70.3 %all-reduce.10.cloned.1.call-done = bf16[2048,256]{0,1:T(8,128)(2,1)} async-done(((bf16[2048,256]{0,1:T(8,128)(2,1)}), bf16[2048,256]{0,1:T(8,128)(2,1)}) %all-reduce.10.cloned.1.call-update) | async-done | bytes 1048592 | tf_op jit(solution)/shard_map/psum | solution.py:109
  306.3 2.6 copy.16
  308.8 223.9 %all-reduce.12.cloned.1.call-done = (f32[3,3,256,512]{2,1,0,3:T(4,128)}, f32[3,3,512,512]{2,1,0,3:T(4,128)}) async-done(((f32[3,3,256,512]{2,1,0,3:T(4,128)}, f32[3,3,512,512]{2,1,0,3:T(4,128)}), (f32[3,3,256,512]{2,1,0,3:T(4,128)}, f32[3,3,512,512]{2,1,0,3:T(4,128)})) %all-reduce.12.cloned.1.call-update) | async-done | bytes 14155792
  532.7 0.8 constant_dynamic-slice_fusion.1
  533.5 0.9 constant_dynamic-slice_fusion
  (112 shorter events, 20.6 us)
Async XLA Ops:
  7.2 1.2 copy-start
  7.2 8.3 %copy-start.2 = (bf16[1,16,32,512]{3,2,1,0:T(8,128)(2,1)S(1)}, bf16[1,16,32,512]{3,2,1,0:T(8,128)(2,1)}, u32[]{:S(2)}) copy-start(bf16[1,16,32,512]{3,2,1,0:T(8,128)(2,1)} %param.9) | copy-start | bytes 1572868
  7.2 94.8 %all-gather.6.cloned.1.call-start = ((), (), s32[]{:S(2)}) async-start(), calls=%async_computation.2 | async-start | bytes 10485760 | tf_op jit(solution)/shard_map/all_gather | solution.py:9
  15.5 176.3 %all-gather.4.cloned.1.call-start = ((), (), s32[]{:S(2)}) async-start(), calls=%async_computation | async-start | bytes 1310720 | tf_op jit(solution)/shard_map/all_gather | solution.py:102
  15.6 9.0 %collective-permute-start.4 = (bf16[1,32,512]{2,1,0:T(8,128)(2,1)S(1)}, bf16[1,32,512]{2,1,0:T(8,128)(2,1)S(1)}, u32[]{:S(2)}, u32[]{:S(2)}) collective-permute-start(bf16[1,32,512]{2,1,0:T(8,128)(2,1)S(1)} %get-tuple-element.40), channel_id=1, source_target_pairs={{0,2},{2,4},{4,6},{6,8},{8,10},{10,12},{12,14},{14,16},{16,18},{18... | collective-permute-start | bytes 98312 | tf_op jit(solution)/shard_map/ppermute | solution.py:17
  19.9 5.6 %collective-permute-start.5 = (bf16[1,32,512]{2,1,0:T(8,128)(2,1)S(1)}, bf16[1,32,512]{2,1,0:T(8,128)(2,1)S(1)}, u32[]{:S(2)}, u32[]{:S(2)}) collective-permute-start(bf16[1,32,512]{2,1,0:T(8,128)(2,1)S(1)} %get-tuple-element.41), channel_id=1, source_target_pairs={{2,0},{4,2},{6,4},{8,6},{10,8},{12,10},{14,12},{16,14},{18,16},{20... | collective-permute-start | bytes 98312 | tf_op jit(solution)/shard_map/ppermute | solution.py:20
  25.9 2.6 copy-start.3
  108.6 8.7 %collective-permute-start = (bf16[1,32,256]{2,1,0:T(8,128)(2,1)S(1)}, bf16[1,32,256]{2,1,0:T(8,128)(2,1)S(1)}, u32[]{:S(2)}, u32[]{:S(2)}) collective-permute-start(bf16[1,32,256]{2,1,0:T(8,128)(2,1)S(1)} %get-tuple-element.54), channel_id=1, source_target_pairs={{0,2},{2,4},{4,6},{6,8},{8,10},{10,12},{12,14},{14,16},{16,18},{18... | collective-permute-start | bytes 49160 | tf_op jit(solution)/shard_map/ppermute | solution.py:17
  111.6 5.7 %collective-permute-start.1 = (bf16[1,32,256]{2,1,0:T(8,128)(2,1)S(1)}, bf16[1,32,256]{2,1,0:T(8,128)(2,1)S(1)}, u32[]{:S(2)}, u32[]{:S(2)}) collective-permute-start(bf16[1,32,256]{2,1,0:T(8,128)(2,1)S(1)} %get-tuple-element.55), channel_id=1, source_target_pairs={{2,0},{4,2},{6,4},{8,6},{10,8},{12,10},{14,12},{16,14},{18,16},{20... | collective-permute-start | bytes 49160 | tf_op jit(solution)/shard_map/ppermute | solution.py:20
  117.2 6.4 %copy-start.19 = (f32[512,512]{1,0:T(8,128)}, f32[512,512]{1,0:T(8,128)S(1)}, u32[]{:S(2)}) copy-start(f32[512,512]{1,0:T(8,128)S(1)} %fusion.4) | copy-start | bytes 3145732
  117.2 2.0 copy-start.6
  122.0 1.6 copy-start.16
  126.4 24.5 %collective-permute-start.2 = (bf16[1,32,512]{2,1,0:T(8,128)(2,1)S(1)}, bf16[1,32,512]{2,1,0:T(8,128)(2,1)S(1)}, u32[]{:S(2)}, u32[]{:S(2)}) collective-permute-start(bf16[1,32,512]{2,1,0:T(8,128)(2,1)S(1)} %get-tuple-element.44), channel_id=1, source_target_pairs={{0,2},{2,4},{4,6},{6,8},{8,10},{10,12},{12,14},{14,16},{16,18},{18... | collective-permute-start | bytes 98312 | tf_op jit(solution)/shard_map/ppermute | solution.py:17
  128.3 22.6 %collective-permute-start.3 = (bf16[1,32,512]{2,1,0:T(8,128)(2,1)S(1)}, bf16[1,32,512]{2,1,0:T(8,128)(2,1)S(1)}, u32[]{:S(2)}, u32[]{:S(2)}) collective-permute-start(bf16[1,32,512]{2,1,0:T(8,128)(2,1)S(1)} %get-tuple-element.45), channel_id=1, source_target_pairs={{2,0},{4,2},{6,4},{8,6},{10,8},{12,10},{14,12},{16,14},{18,16},{20... | collective-permute-start | bytes 98312 | tf_op jit(solution)/shard_map/ppermute | solution.py:20
  133.2 19.6 %collective-permute-start.6 = (bf16[1,32,512]{2,1,0:T(8,128)(2,1)S(1)}, bf16[1,32,512]{2,1,0:T(8,128)(2,1)S(1)}, u32[]{:S(2)}, u32[]{:S(2)}) collective-permute-start(bf16[1,32,512]{2,1,0:T(8,128)(2,1)S(1)} %get-tuple-element.36), channel_id=1, source_target_pairs={{0,2},{2,4},{4,6},{6,8},{8,10},{10,12},{12,14},{14,16},{16,18},{18... | collective-permute-start | bytes 98312 | tf_op jit(solution)/shard_map/ppermute | solution.py:17
  135.1 17.7 %collective-permute-start.7 = (bf16[1,32,512]{2,1,0:T(8,128)(2,1)S(1)}, bf16[1,32,512]{2,1,0:T(8,128)(2,1)S(1)}, u32[]{:S(2)}, u32[]{:S(2)}) collective-permute-start(bf16[1,32,512]{2,1,0:T(8,128)(2,1)S(1)} %get-tuple-element.37), channel_id=1, source_target_pairs={{2,0},{4,2},{6,4},{8,6},{10,8},{12,10},{14,12},{16,14},{18,16},{20... | collective-permute-start | bytes 98312 | tf_op jit(solution)/shard_map/ppermute | solution.py:20
  153.1 1.7 copy-start.7
  155.2 1.2 copy-start.17
  155.2 1.5 copy-start.20
  159.4 146.9 %all-reduce.10.cloned.1.call-start = ((), (), s32[]{:S(2)}) async-start(), calls=%async_computation.1 | async-start | bytes 2097152 | tf_op jit(solution)/shard_map/psum | solution.py:109
  159.5 0.8 copy-start.14
  159.5 2.3 copy-start.8
  161.8 1.9 copy-start.9
  162.3 1.9 copy-start.10
  163.7 1.0 copy-start.13
  164.2 1.1 copy-start.11
  164.7 2.0 copy-start.21
  198.8 333.9 %all-reduce.12.cloned.1.call-start = ((), (), s32[]{:S(2)}) async-start(), calls=%async_computation.3 | async-start | bytes 37748736
  199.1 2.8 copy-start.4
  199.1 3.8 copy-start.5
  221.3 1.7 copy-start.12
  221.3 3.2 copy-start.15
  227.5 1.6 copy-start.18
  233.6 302.1 %copy-start.1 = (bf16[2048,256]{1,0:T(8,128)(2,1)S(1)}, bf16[2048,256]{1,0:T(8,128)(2,1)}, u32[]{:S(2)}) copy-start(bf16[2048,256]{1,0:T(8,128)(2,1)} %param.6) | copy-start | bytes 3145732
Sparse Core Ops, SparseCore 0:
  15.6 86.3 all-gather.5
  159.5 32.2 all-gather.3
  198.9 107.2 all-reduce.9
  311.7 220.9 all-reduce.11
